TPU v7x, 32 devices: a whole 2x2x4 slice. The times are simulated.
32 devices in a mesh: grp: 4 (over y, core), row: 8 (over z, x).
Axes of the slice: x: 2, y: 2, z: 4, core: 2. Of those that a mesh axis runs over, the one named last changes fastest.
Arguments:
- grad: float32 [32, 2048, 512], P('grp', 'row')
- weight: bfloat16 [32, 2048, 512], P('grp', 'row'), may hold values from -0.125 to 0.125
- owner: int32 [32, 1], P('grp'), may hold values from 0 to 7; in each aligned block of 8 rows (0 to 7, 8 to 15, ...) at most 2 rows name the same one
- tokens: bfloat16 [3072, 2048], P('row'), may hold values from -6 to 6
- counts: int32 [8], P('row'), may hold values from 96 to 384, as said below
Outputs:
- new_weight: bfloat16 [32, 2048, 512], P('grp', 'row')
- mixed: bfloat16 [3072, 512], P('row', 'grp')
Inputs may be any that keep to these rules, and one draw needn't show every extreme that they name: Within each group's 8 consecutive matrices no owner is named more than 2 times, a bound that some block reaches. `counts`: some row index has all 384 rows live.
All inputs are finite; a program needn't handle non-finite values.
Results may differ from a plain program's by a relative error of at most 0.017.
Values may be sent and summed in bfloat16 or wider, within the bound.
A program may use at most 128 MiB of HBM per device.

v0:
```python
import jax
import jax.numpy as jnp
from jax import lax
from jax.sharding import PartitionSpec as P

ITERS = 5
MOST = 2


coef_a = 3.4445
coef_b = -4.775
coef_c = 2.0315
step_size = 0.5


def newton_schulz(start):
    iterate_state = start
    for turn in range(ITERS):
        gram_product = jnp.einsum(
            "jqz,jqa->jza", iterate_state, iterate_state, preferred_element_type=jnp.float32
        ).astype(jnp.bfloat16)
        square = jnp.einsum(
            "kfg,kgj->kfj", gram_product, gram_product, preferred_element_type=jnp.float32
        )
        polynomial_term = (coef_b * gram_product.astype(jnp.float32) + coef_c * square).astype(
            jnp.bfloat16
        )
        weight_update = jnp.einsum(
            "yon,ynb->yob", iterate_state, polynomial_term, preferred_element_type=jnp.float32
        )
        iterate_state = (coef_a * iterate_state.astype(jnp.float32) + weight_update).astype(
            jnp.bfloat16
        )
    return iterate_state


def body(grad, weight, owner, tokens, counts):
    ranks = lax.axis_size("row")
    groups = lax.axis_size("grp")
    number = grad.shape[0]
    rows = grad.shape[1]
    width = grad.shape[2]
    local = jnp.sum(grad * grad, axis=(1, 2))
    norm2 = lax.psum(local, "row")
    start = (grad / (jnp.sqrt(norm2) + 1e-07)[:, None, None]).astype(jnp.bfloat16)
    target = owner[:, 0]
    before = jnp.arange(number)[None, :] < jnp.arange(number)[:, None]
    same = target[None, :] == target[:, None]
    slot = jnp.sum((same & before).astype(jnp.int32), axis=1)
    place = target * MOST + slot
    table = (jnp.arange(ranks * MOST)[:, None] == place[None, :]).astype(jnp.bfloat16)

    def assemble(piece):
        count = piece.shape[1]
        return piece.transpose(1, 0, 2, 3).reshape(count, ranks * rows, width)

    ortho = newton_schulz(
        assemble(lax.all_to_all(start[:, None], "row", split_axis=0, concat_axis=0, tiled=True))
    )
    old = assemble(lax.all_to_all(weight[:, None], "row", split_axis=0, concat_axis=0, tiled=True))
    whole = (old.astype(jnp.float32) - step_size * ortho.astype(jnp.float32)).astype(jnp.bfloat16)
    count = whole.shape[0]
    solved = whole.reshape(count, ranks, rows, width).transpose(1, 0, 2, 3)
    returned_output = lax.all_to_all(solved, "row", split_axis=0, concat_axis=0, tiled=True)
    new_weight = returned_output[:, 0]
    moved = jnp.dot(
        table, new_weight.reshape(number, rows * width), preferred_element_type=jnp.float32
    )
    partial_output = jnp.einsum(
        "ix,oxv->iov",
        tokens,
        assemble(
            lax.all_to_all(
                moved.astype(jnp.bfloat16).reshape(ranks, MOST, rows, width),
                "row",
                split_axis=0,
                concat_axis=0,
                tiled=True,
            )
        ),
        preferred_element_type=jnp.float32,
    )
    proj = jnp.sum(partial_output, axis=1) * groups ** (-0.5)
    summed = lax.psum_scatter(
        proj.astype(jnp.bfloat16), "grp", scatter_dimension=1, tiled=True
    ).astype(jnp.float32)
    live = jnp.arange(summed.shape[0])[:, None] < counts[0]
    mixed = jnp.where(live, summed, 0.0).astype(jnp.bfloat16)
    return (new_weight, mixed)


def solution(mesh):
    placed = (
        P("grp", "row", None),
        P("grp", "row", None),
        P("grp", None),
        P("row", None),
        P("row"),
    )
    return jax.shard_map(
        body,
        mesh=mesh,
        in_specs=placed,
        out_specs=(P("grp", "row", None), P("row", "grp")),
        check_vma=False,
    )
```

profile of v0, /device:TPU:8, one launch (start us, length us, event | category | flops | bytes accessed | tf_op | source)
XLA Modules:
  0.0 345.7 jit_solution(1346113802811700175)
XLA Ops:
  7.2 0.0 copy-start
  7.2 2.7 multiply_reduce_fusion
  9.9 18.8 %psum.7 = f32[8]{0:T(128)S(1)} all-reduce(f32[8]{0:T(128)S(1)} %multiply_reduce_fusion), channel_id=1, replica_groups=mesh['grp'=4,'row'=8] {'row'}, use_global_device_ids=true, to_apply=%region_1.0 | all-reduce | flops 8 | bytes 64 | tf_op jit(solution)/shard_map/psum | solution.py:44
  28.8 2.8 fusion.3
  31.6 50.3 %all_to_all.20 = bf16[8,1,256,512]{3,2,1,0:T(8,128)(2,1)} all-to-all(bf16[8,1,256,512]{3,2,1,0:T(8,128)(2,1)S(1)} %fusion.3), channel_id=1, replica_groups=mesh['grp'=4,'row'=8] {'row'}, dimensions={0} | all-to-all | bytes 4194304 | tf_op jit(solution)/shard_map/all_to_all | solution.py:58
  81.9 5.1 %all-to-all-start = ((bf16[8,1,256,512]{3,2,1,0:T(8,128)(2,1)}), bf16[8,1,256,512]{3,2,1,0:T(8,128)(2,1)}, u32[]{:S(2)}, u32[]{:S(2)}) async-start(bf16[8,1,256,512]{3,2,1,0:T(8,128)(2,1)} %bitcast.74), calls=%async_computation | async-start | bytes 4194304 | tf_op jit(solution)/shard_map/all_to_all | solution.py:60
  87.0 3.5 %fusion.22 = bf16[512,512]{1,0:T(8,128)(2,1)S(1)} fusion(bf16[8,1,256,512]{3,2,1,0:T(8,128)(2,1)} %all_to_all.20), kind=kOutput, calls=%fused_computation.32 | convolution fusion | flops 1074003968 | bytes 2621440 | tf_op jit(solution)/shard_map/jqz,jqa->jza/dot_general | solution.py:19
  90.5 5.2 %add_convert_fusion.4 = bf16[2048,512]{1,0:T(8,128)(2,1)} fusion(bf16[2048,512]{1,0:T(8,128)(2,1)} %bitcast.76, bf16[512,512]{1,0:T(8,128)(2,1)S(1)} %fusion.22), kind=kOutput, calls=%fused_computation.7 | convolution fusion | flops 1347682304 | bytes 4718592 | tf_op jit(solution)/shard_map/yon,ynb->yob/dot_general | solution.py:28
  95.7 3.5 %convolution_convert_fusion.4 = bf16[512,512]{1,0:T(8,128)(2,1)S(1)} fusion(bf16[2048,512]{1,0:T(8,128)(2,1)} %add_convert_fusion.4), kind=kOutput, calls=%fused_computation.36 | convolution fusion | flops 1074003968 | bytes 2621440 | tf_op jit(solution)/shard_map/jqz,jqa->jza/dot_general | solution.py:19
  99.2 5.1 %add_convert_fusion.3 = bf16[2048,512]{1,0:T(8,128)(2,1)} fusion(bf16[2048,512]{1,0:T(8,128)(2,1)} %add_convert_fusion.4, bf16[512,512]{1,0:T(8,128)(2,1)S(1)} %convolution_convert_fusion.4), kind=kOutput, calls=%fused_computation.6 | convolution fusion | flops 1347682304 | bytes 4718592 | tf_op jit(solution)/shard_map/yon,ynb->yob/dot_general | solution.py:28
  104.3 3.5 %convolution_convert_fusion.3 = bf16[512,512]{1,0:T(8,128)(2,1)S(1)} fusion(bf16[2048,512]{1,0:T(8,128)(2,1)} %add_convert_fusion.3), kind=kOutput, calls=%fused_computation.35 | convolution fusion | flops 1074003968 | bytes 2621440 | tf_op jit(solution)/shard_map/jqz,jqa->jza/dot_general | solution.py:19
  107.8 5.2 %add_convert_fusion.2 = bf16[2048,512]{1,0:T(8,128)(2,1)} fusion(bf16[2048,512]{1,0:T(8,128)(2,1)} %add_convert_fusion.3, bf16[512,512]{1,0:T(8,128)(2,1)S(1)} %convolution_convert_fusion.3), kind=kOutput, calls=%fused_computation.5 | convolution fusion | flops 1347682304 | bytes 4718592 | tf_op jit(solution)/shard_map/yon,ynb->yob/dot_general | solution.py:28
  113.0 3.5 %convolution_convert_fusion.2 = bf16[512,512]{1,0:T(8,128)(2,1)S(1)} fusion(bf16[2048,512]{1,0:T(8,128)(2,1)} %add_convert_fusion.2), kind=kOutput, calls=%fused_computation.34 | convolution fusion | flops 1074003968 | bytes 2621440 | tf_op jit(solution)/shard_map/jqz,jqa->jza/dot_general | solution.py:19
  116.5 5.1 %add_convert_fusion.1 = bf16[2048,512]{1,0:T(8,128)(2,1)} fusion(bf16[2048,512]{1,0:T(8,128)(2,1)} %add_convert_fusion.2, bf16[512,512]{1,0:T(8,128)(2,1)S(1)} %convolution_convert_fusion.2), kind=kOutput, calls=%fused_computation.4 | convolution fusion | flops 1347682304 | bytes 4718592 | tf_op jit(solution)/shard_map/yon,ynb->yob/dot_general | solution.py:28
  121.6 3.5 %convolution_convert_fusion.1 = bf16[512,512]{1,0:T(8,128)(2,1)S(1)} fusion(bf16[2048,512]{1,0:T(8,128)(2,1)} %add_convert_fusion.1), kind=kOutput, calls=%fused_computation.33 | convolution fusion | flops 1074003968 | bytes 2621440 | tf_op jit(solution)/shard_map/jqz,jqa->jza/dot_general | solution.py:19
  125.1 4.9 %all-to-all-done = bf16[8,1,256,512]{3,2,1,0:T(8,128)(2,1)} async-done(((bf16[8,1,256,512]{3,2,1,0:T(8,128)(2,1)}), bf16[8,1,256,512]{3,2,1,0:T(8,128)(2,1)}, u32[]{:S(2)}, u32[]{:S(2)}) %all-to-all-start) | async-done | bytes 2097184 | tf_op jit(solution)/shard_map/all_to_all | solution.py:60
  130.0 5.6 %fusion = bf16[2048,512]{1,0:T(8,128)(2,1)} fusion(bf16[2048,512]{1,0:T(8,128)(2,1)} %bitcast.16, bf16[2048,512]{1,0:T(8,128)(2,1)} %add_convert_fusion.1, bf16[512,512]{1,0:T(8,128)(2,1)S(1)} %convolution_convert_fusion.1), kind=kOutput, calls=%fused_computation.2 | convolution fusion | flops 1352925184 | bytes 6815744 | tf_op jit(solution)/shard_map/yon,ynb->yob/dot_general | solution.py:28
  135.6 0.0 copy-start.1
  135.6 8.1 %all-to-all-start.2 = ((bf16[8,1,256,512]{3,2,1,0:T(8,128)(2,1)}), bf16[8,1,256,512]{3,2,1,0:T(8,128)(2,1)}, u32[]{:S(2)}, u32[]{:S(2)}) async-start(bf16[8,1,256,512]{3,2,1,0:T(8,128)(2,1)} %bitcast.75), calls=%async_computation.2 | async-start | bytes 4194304 | tf_op jit(solution)/shard_map/all_to_all | solution.py:64
  143.7 0.0 reduce-scatter.4.cloned.1.call-start
  143.7 0.0 copy-done.1
  143.7 0.2 convert_reduce_fusion
  143.9 44.7 %all-to-all-done.2 = bf16[8,1,256,512]{3,2,1,0:T(8,128)(2,1)} async-done(((bf16[8,1,256,512]{3,2,1,0:T(8,128)(2,1)}), bf16[8,1,256,512]{3,2,1,0:T(8,128)(2,1)}, u32[]{:S(2)}, u32[]{:S(2)}) %all-to-all-start.2) | async-done | bytes 2097184 | tf_op jit(solution)/shard_map/all_to_all | solution.py:64
  188.6 2.8 copy.20
  191.4 1.2 convolution_convert_fusion
  192.6 1.4 copy.21
  194.1 98.8 %all_to_all.21 = bf16[8,2,256,512]{3,2,1,0:T(8,128)(2,1)} all-to-all(bf16[8,2,256,512]{3,2,1,0:T(8,128)(2,1)S(1)} %bitcast.71), channel_id=1, replica_groups=mesh['grp'=4,'row'=8] {'row'}, dimensions={0} | all-to-all | bytes 8388608 | tf_op jit(solution)/shard_map/all_to_all | solution.py:73
  292.8 8.0 %copy.15 = bf16[2,8,256,512]{2,1,3,0:T(8,128)(2,1)} copy(bf16[2,8,256,512]{3,2,0,1:T(8,128)(2,1)} %bitcast.72) | data formatting | bytes 8388608 | tf_op jit(solution)/shard_map/transpose | solution.py:55
  300.8 7.4 %reshape.166 = bf16[2,2048,512]{1,2,0:T(8,128)(2,1)} reshape(bf16[2,8,256,512]{2,1,3,0:T(8,128)(2,1)} %copy.15) | data formatting | bytes 8388608 | tf_op jit(solution)/shard_map/reshape | solution.py:55
  308.2 0.0 copy-done
  308.2 4.6 %fusion.6 = f32[512,384]{1,0:T(8,128)S(1)} fusion(bf16[2,2048,512]{1,2,0:T(8,128)(2,1)} %reshape.166, bf16[384,2048]{1,0:T(8,128)(2,1)S(1)} %copy-done), kind=kOutput, calls=%fused_computation.15 | convolution fusion | flops 1610809344 | bytes 6553600 | tf_op jit(solution)/shard_map/ix,oxv->iov/dot_general | solution.py:69
  312.8 0.8 multiply_convert_fusion
  313.6 0.0 reduce-scatter.4.cloned.1.call-update
  314.3 19.8 %reduce-scatter.4.cloned.1.call-done = bf16[128,384]{1,0:T(8,128)(2,1)} async-done(((bf16[512,384]{1,0:T(8,128)(2,1)}), bf16[128,384]{1,0:T(8,128)(2,1)}) %reduce-scatter.4.cloned.1.call-update) | async-done | bytes 98320
  334.1 1.0 copy.19
  335.1 0.8 select_convert_fusion
  335.8 3.0 copy.24
  (3 shorter events, 0.0 us)
Async XLA Ops:
  7.2 301.0 %copy-start = (bf16[384,2048]{1,0:T(8,128)(2,1)S(1)}, bf16[384,2048]{1,0:T(8,128)(2,1)}, u32[]{:S(2)}) copy-start(bf16[384,2048]{1,0:T(8,128)(2,1)} %param.8) | copy-start | bytes 4718596
  81.9 48.1 %all-to-all-start = ((bf16[8,1,256,512]{3,2,1,0:T(8,128)(2,1)}), bf16[8,1,256,512]{3,2,1,0:T(8,128)(2,1)}, u32[]{:S(2)}, u32[]{:S(2)}) async-start(bf16[8,1,256,512]{3,2,1,0:T(8,128)(2,1)} %bitcast.74), calls=%async_computation | async-start | bytes 4194304 | tf_op jit(solution)/shard_map/all_to_all | solution.py:60
  135.6 8.1 %copy-start.1 = (s32[8,1]{0,1:T(1,128)S(1)}, s32[8,1]{0,1:T(1,128)}, u32[]{:S(2)}) copy-start(s32[8,1]{0,1:T(1,128)} %param.7) | copy-start | bytes 100
  135.6 53.1 %all-to-all-start.2 = ((bf16[8,1,256,512]{3,2,1,0:T(8,128)(2,1)}), bf16[8,1,256,512]{3,2,1,0:T(8,128)(2,1)}, u32[]{:S(2)}, u32[]{:S(2)}) async-start(bf16[8,1,256,512]{3,2,1,0:T(8,128)(2,1)} %bitcast.75), calls=%async_computation.2 | async-start | bytes 4194304 | tf_op jit(solution)/shard_map/all_to_all | solution.py:64
  143.7 190.4 %reduce-scatter.4.cloned.1.call-start = ((), (), s32[]{:S(2)}) async-start(), calls=%async_computation.5 | async-start | bytes 491520
Sparse Core Ops, SparseCore 0:
  313.8 20.2 reduce-scatter.3
where the time goes:
time: 348 us; the launch traced here: 346 us
  blocking collectives  168 us (48%)
  waiting for transfers between devices  69.4 us (20%)
  matrix products  49.4 us (14%)
  local copies, waits for them, and re-layouts  23.6 us (7%)
  between operations  14.8 us (4%)
  starting transfers between devices  13.3 us (4%)
  other arithmetic  7.35 us (2%)
    all_to_all x1, blocking collectives, body(): lax.all_to_all(moved.astype(jnp.bfloat16).reshape(ranks, MOST, rows, widt...  98.8 us
    all_to_all x1, blocking collectives, body(): lax.all_to_all(start[:, None], 'row', split_axis=0, concat_axis=0, tiled=...  50.3 us
    all_to_all x1, waiting for transfers between devices, body(): lax.all_to_all(solved, 'row', split_axis=0, concat_axis=0, tiled=True)  44.7 us
    dot_general x5, matrix products, newton_schulz(): jnp.einsum('yon,ynb->yob', iterate_state, polynomial_term, preferred_elem...  26.1 us
    unnamed x2, waiting for transfers between devices  19.8 us
    psum x1, blocking collectives, body(): norm2 = lax.psum(local, 'row')  18.8 us
    dot_general x5, matrix products, newton_schulz(): jnp.einsum('jqz,jqa->jza', iterate_state, iterate_state, preferred_elemen...  17.4 us
    unnamed x8, local copies, waits for them, and re-layouts  8.25 us
  transfers between devices with their start and end apart: 3, of which 3 were waited for; matrix products, arithmetic and copies ran while one was open for 11% of the time, Pallas kernels for 0%

commit v1 on v0

v1 whole, which is shorter than its diff:
```python
import jax
import jax.numpy as jnp
from jax import lax
from jax.sharding import PartitionSpec as P

ITERS = 5
MOST = 2

coef_a = 3.4445
coef_b = -4.775
coef_c = 2.0315
step_size = 0.5

f32 = jnp.float32
bf16 = jnp.bfloat16


def newton_schulz(raw):
    x32 = raw.astype(f32)
    norm2 = jnp.sum(x32 * x32)
    scale = 1.0 / (jnp.sqrt(norm2) + 1e-07)
    state = raw
    for turn in range(ITERS):
        gram = jnp.dot(state.T, state, preferred_element_type=f32)
        if turn == 0:
            gram = jnp.where(norm2 < jnp.inf, scale * (scale * gram), 0.0)
        gram = gram.astype(bf16)
        square = jnp.dot(gram, gram, preferred_element_type=f32)
        poly = (coef_b * gram.astype(f32) + coef_c * square).astype(bf16)
        update = jnp.dot(state, poly, preferred_element_type=f32)
        if turn == 0:
            state = ((coef_a * scale) * state.astype(f32) + scale * update).astype(bf16)
        else:
            state = (coef_a * state.astype(f32) + update).astype(bf16)
    return state


def body(grad, weight, owner, tokens, counts):
    ranks = lax.axis_size("row")
    groups = lax.axis_size("grp")
    number, rows, width = grad.shape
    top = float(jnp.finfo(bf16).max)
    raw = jnp.clip(grad, -top, top).astype(bf16)
    assert number == ranks
    whole = lax.all_to_all(raw, "row", split_axis=0, concat_axis=0, tiled=True)

    count = tokens.shape[0]
    part = count // groups
    mine = lax.dynamic_slice_in_dim(tokens, lax.axis_index("grp") * part, part, 0)
    mine = mine.reshape(part, ranks, rows).transpose(1, 0, 2)
    moved = lax.all_to_all(mine, "row", split_axis=0, concat_axis=0, tiled=True)
    cols = lax.all_gather(moved, "grp", axis=1, tiled=True)

    ortho = newton_schulz(whole.reshape(ranks * rows, width))
    back = lax.all_to_all(
        ortho.reshape(ranks, rows, width), "row", split_axis=0, concat_axis=0, tiled=True
    )
    new_weight = (weight.astype(f32) - step_size * back.astype(f32)).astype(bf16)

    target = owner[:, 0]
    before = jnp.arange(number)[None, :] < jnp.arange(number)[:, None]
    same = target[None, :] == target[:, None]
    slot = jnp.sum((same & before).astype(jnp.int32), axis=1)
    hit = (target[None, None, :] == jnp.arange(ranks)[:, None, None]) & (
        slot[None, None, :] == jnp.arange(MOST)[None, :, None]
    )
    index = jnp.sum(hit * jnp.arange(number)[None, None, :], axis=2)
    valid = jnp.any(hit, axis=2)
    total = 0.0
    for s in range(MOST):
        picked = jnp.take(new_weight, index[:, s], axis=0)
        picked = jnp.where(valid[:, s][:, None, None], picked, jnp.zeros_like(picked))
        picked = picked.reshape(ranks, rows, groups, width // groups)
        total = total + jnp.einsum("bti,bigc->gbtc", cols, picked, preferred_element_type=f32)
    proj = (total * groups ** (-0.5)).astype(bf16)
    proj = proj.reshape(groups * ranks, count, width // groups)
    summed = lax.psum_scatter(proj, ("grp", "row"), scatter_dimension=0, tiled=True)[0]
    live = jnp.arange(count)[:, None] < counts[0]
    mixed = jnp.where(live, summed, jnp.zeros_like(summed))
    return (new_weight, mixed)


def solution(mesh):
    placed = (
        P("grp", "row", None),
        P("grp", "row", None),
        P("grp", None),
        P("row", None),
        P("row"),
    )
    return jax.shard_map(
        body,
        mesh=mesh,
        in_specs=placed,
        out_specs=(P("grp", "row", None), P("row", "grp")),
        check_vma=False,
    )
```

time: 348 us -> 319 us (0.917)
  blocking collectives: 168 us -> 0 us
  waiting for transfers between devices: 69.4 us -> 192 us
  other arithmetic: 7.35 us -> 18.3 us
  starting transfers between devices: 13.3 us -> 18.7 us
    all_to_all x2 -> x0, blocking collectives: 149 us -> none  [the longest x1 98.8 us: body(): lax.all_to_all(moved.astype(jnp.bfloat16).reshape(ranks, MOST, rows, widt...]
    reduce_scatter x0 -> x1, waiting for transfers between devices: none -> 103 us  [body(): lax.psum_scatter(proj, ('grp', 'row'), scatter_dimension=0, tiled=True)[0]]
    all_to_all x2 -> x3, waiting for transfers between devices: 49.7 us -> 88.9 us  [the longest x1 45 us: body(): whole = lax.all_to_all(raw, 'row', split_axis=0, concat_axis=0, tiled=True)]
    unnamed x2, waiting for transfers between devices: 19.8 us -> 0.73 us
    psum x1 -> x0, blocking collectives: 18.8 us -> none  [body(): norm2 = lax.psum(local, 'row')]
    transpose x1 -> x0, local copies, waits for them, and re-layouts: 7.98 us -> none  [assemble(): return piece.transpose(1, 0, 2, 3).reshape(count, ranks * rows, width)]
    unnamed x8 -> x10, local copies, waits for them, and re-layouts: 8.25 us -> 0.78 us
    gather x0 -> x2, local copies, waits for them, and re-layouts: none -> 7.16 us  [body(): picked = jnp.take(new_weight, index[:, s], axis=0)]
  transfers between devices with their start and end apart: 3 -> 5, of which waited for: 3 -> 3; matrix products, arithmetic and copies ran while one was open for 11% -> 23% of each run, Pallas kernels for 0% -> 0%
where the time goes in v1:
time: 319 us; the launch traced here: 316 us
  waiting for transfers between devices  192 us (60%)
  matrix products  49.8 us (16%)
  local copies, waits for them, and re-layouts  21.2 us (7%)
  starting transfers between devices  18.7 us (6%)
  other arithmetic  18.3 us (6%)
  between operations  16.2 us (5%)
    reduce_scatter x1, waiting for transfers between devices, body(): lax.psum_scatter(proj, ('grp', 'row'), scatter_dimension=0, tiled=True)[0]  103 us
    all_to_all x1, waiting for transfers between devices, body(): whole = lax.all_to_all(raw, 'row', split_axis=0, concat_axis=0, tiled=True)  45 us
    all_to_all x1, waiting for transfers between devices, body(): lax.all_to_all(ortho.reshape(ranks, rows, width), 'row', split_axis=0, co...  43.9 us
    dot_general x5, matrix products, newton_schulz(): update = jnp.dot(state, poly, preferred_element_type=f32)  25.9 us
    dot_general x5, matrix products, newton_schulz(): gram = jnp.dot(state.T, state, preferred_element_type=f32)  17.5 us
    reshape x2, local copies, waits for them, and re-layouts, body(): picked = picked.reshape(ranks, rows, groups, width // groups)  7.79 us
    gather x2, local copies, waits for them, and re-layouts, body(): picked = jnp.take(new_weight, index[:, s], axis=0)  7.16 us
    dot_general x2, matrix products, body(): jnp.einsum('bti,bigc->gbtc', cols, picked, preferred_element_type=f32)  6.38 us
  transfers between devices with their start and end apart: 5, of which 3 were waited for; matrix products, arithmetic and copies ran while one was open for 23% of the time, Pallas kernels for 0%

profile of v1, /device:TPU:8, one launch (start us, length us, event | category | flops | bytes accessed | tf_op | source)
XLA Modules:
  0.0 316.4 jit_solution(2602183782174952777)
XLA Ops:
  7.2 0.0 copy-start
  7.2 3.9 %clamp_convert_fusion = bf16[8,256,512]{2,1,0:T(8,128)(2,1)} fusion(f32[8,256,512]{2,1,0:T(8,128)} %param.7), kind=kLoop, calls=%fused_computation.10 | loop fusion | flops 1048576 | bytes 6291456 | tf_op jit(solution)/shard_map/convert_element_type | solution.py:43
  11.0 6.3 %all-to-all-start = ((bf16[8,256,512]{2,1,0:T(8,128)(2,1)}), bf16[8,256,512]{2,1,0:T(8,128)(2,1)}, u32[]{:S(2)}, u32[]{:S(2)}) async-start(bf16[8,256,512]{2,1,0:T(8,128)(2,1)} %clamp_convert_fusion), calls=%async_computation | async-start | bytes 4194304 | tf_op jit(solution)/shard_map/all_to_all | solution.py:45
  17.3 0.0 copy-done
  17.3 0.8 copy.26
  18.1 45.0 %all-to-all-done = bf16[8,256,512]{2,1,0:T(8,128)(2,1)} async-done(((bf16[8,256,512]{2,1,0:T(8,128)(2,1)}), bf16[8,256,512]{2,1,0:T(8,128)(2,1)}, u32[]{:S(2)}, u32[]{:S(2)}) %all-to-all-start) | async-done | bytes 2097184 | tf_op jit(solution)/shard_map/all_to_all | solution.py:45
  63.1 6.2 %all-to-all-start.2 = ((bf16[8,96,256]{2,1,0:T(8,128)(2,1)}), bf16[8,96,256]{2,1,0:T(8,128)(2,1)S(1)}, u32[]{:S(2)}, u32[]{:S(2)}) async-start(bf16[8,96,256]{2,1,0:T(8,128)(2,1)} %bitcast.71), calls=%async_computation.2 | async-start | bytes 786432 | tf_op jit(solution)/shard_map/all_to_all | solution.py:51
  69.3 3.3 %multiply_reduce_fusion = f32[]{:T(128)} fusion(bf16[8,256,512]{2,1,0:T(8,128)(2,1)} %all-to-all-done), kind=kLoop, calls=%fused_computation.9 | loop fusion | flops 3145727 | bytes 2097156 | tf_op jit(solution)/shard_map/reduce_sum | solution.py:20
  73.9 3.5 %fusion.12 = bf16[512,512]{1,0:T(8,128)(2,1)S(1)} fusion(bf16[8,256,512]{2,1,0:T(8,128)(2,1)} %all-to-all-done, f32[]{:T(128)S(6)} %div.3, pred[]{:T(512)S(6)} %lt.33), kind=kOutput, calls=%fused_computation.31 | convolution fusion | flops 1074790400 | bytes 2621445 | tf_op jit(solution)/shard_map/dot_general | solution.py:24
  77.4 5.3 %add_convert_fusion.4 = bf16[2048,512]{1,0:T(8,128)(2,1)} fusion(bf16[2048,512]{1,0:T(8,128)(2,1)} %bitcast, f32[]{:T(128)S(6)} %div.3, f32[]{:T(128)S(6)} %mul.96, bf16[512,512]{1,0:T(8,128)(2,1)S(1)} %fusion.12), kind=kOutput, calls=%fused_computation.8 | convolution fusion | flops 1348730880 | bytes 4718600 | tf_op jit(solution)/shard_map/dot_general | solution.py:30
  82.7 3.5 %convolution_convert_fusion.3 = bf16[512,512]{1,0:T(8,128)(2,1)S(1)} fusion(bf16[2048,512]{1,0:T(8,128)(2,1)} %add_convert_fusion.4), kind=kOutput, calls=%fused_computation.40 | convolution fusion | flops 1074003968 | bytes 2621440 | tf_op jit(solution)/shard_map/dot_general | solution.py:24
  86.2 5.2 %add_convert_fusion.3 = bf16[2048,512]{1,0:T(8,128)(2,1)} fusion(bf16[2048,512]{1,0:T(8,128)(2,1)} %add_convert_fusion.4, bf16[512,512]{1,0:T(8,128)(2,1)S(1)} %convolution_convert_fusion.3), kind=kOutput, calls=%fused_computation.7 | convolution fusion | flops 1347682304 | bytes 4718592 | tf_op jit(solution)/shard_map/dot_general | solution.py:30
  91.4 3.5 %convolution_convert_fusion.2 = bf16[512,512]{1,0:T(8,128)(2,1)S(1)} fusion(bf16[2048,512]{1,0:T(8,128)(2,1)} %add_convert_fusion.3), kind=kOutput, calls=%fused_computation.39 | convolution fusion | flops 1074003968 | bytes 2621440 | tf_op jit(solution)/shard_map/dot_general | solution.py:24
  94.9 5.2 %add_convert_fusion.2 = bf16[2048,512]{1,0:T(8,128)(2,1)} fusion(bf16[2048,512]{1,0:T(8,128)(2,1)} %add_convert_fusion.3, bf16[512,512]{1,0:T(8,128)(2,1)S(1)} %convolution_convert_fusion.2), kind=kOutput, calls=%fused_computation.6 | convolution fusion | flops 1347682304 | bytes 4718592 | tf_op jit(solution)/shard_map/dot_general | solution.py:30
  100.0 3.5 %convolution_convert_fusion.1 = bf16[512,512]{1,0:T(8,128)(2,1)S(1)} fusion(bf16[2048,512]{1,0:T(8,128)(2,1)} %add_convert_fusion.2), kind=kOutput, calls=%fused_computation.38 | convolution fusion | flops 1074003968 | bytes 2621440 | tf_op jit(solution)/shard_map/dot_general | solution.py:24
  103.5 5.2 %add_convert_fusion.1 = bf16[2048,512]{1,0:T(8,128)(2,1)} fusion(bf16[2048,512]{1,0:T(8,128)(2,1)} %add_convert_fusion.2, bf16[512,512]{1,0:T(8,128)(2,1)S(1)} %convolution_convert_fusion.1), kind=kOutput, calls=%fused_computation.5 | convolution fusion | flops 1347682304 | bytes 4718592 | tf_op jit(solution)/shard_map/dot_general | solution.py:30
  108.7 3.5 %convolution_convert_fusion = bf16[512,512]{1,0:T(8,128)(2,1)S(1)} fusion(bf16[2048,512]{1,0:T(8,128)(2,1)} %add_convert_fusion.1), kind=kOutput, calls=%fused_computation.37 | convolution fusion | flops 1074003968 | bytes 2621440 | tf_op jit(solution)/shard_map/dot_general | solution.py:24
  112.2 5.2 %add_convert_fusion = bf16[2048,512]{1,0:T(8,128)(2,1)} fusion(bf16[2048,512]{1,0:T(8,128)(2,1)} %add_convert_fusion.1, bf16[512,512]{1,0:T(8,128)(2,1)S(1)} %convolution_convert_fusion), kind=kOutput, calls=%fused_computation.4 | convolution fusion | flops 1347682304 | bytes 4718592 | tf_op jit(solution)/shard_map/dot_general | solution.py:30
  117.4 0.0 all-to-all-done.2
  117.4 0.0 copy-start.3
  117.4 0.0 copy-start.4
  117.4 0.8 copy-done.3
  118.1 6.0 %all-to-all-start.1 = ((bf16[8,256,512]{2,1,0:T(8,128)(2,1)}), bf16[8,256,512]{2,1,0:T(8,128)(2,1)}, u32[]{:S(2)}, u32[]{:S(2)}) async-start(bf16[8,256,512]{2,1,0:T(8,128)(2,1)} %bitcast.76), calls=%async_computation.1 | async-start | bytes 4194304 | tf_op jit(solution)/shard_map/all_to_all | solution.py:55
  124.1 0.0 all-gather.2.cloned.1.call-start
  124.1 0.7 all-gather.2.cloned.1.call-update
  124.9 0.2 reduce-scatter.2.cloned.1.call-start
  125.1 0.0 copy-done.4
  125.1 0.2 convert_reduce_fusion
  125.3 0.1 fusion.28
  125.5 0.1 and_reduce_fusion
  125.6 43.9 %all-to-all-done.1 = bf16[8,256,512]{2,1,0:T(8,128)(2,1)} async-done(((bf16[8,256,512]{2,1,0:T(8,128)(2,1)}), bf16[8,256,512]{2,1,0:T(8,128)(2,1)}, u32[]{:S(2)}, u32[]{:S(2)}) %all-to-all-start.1) | async-done | bytes 2097184 | tf_op jit(solution)/shard_map/all_to_all | solution.py:55
  169.5 4.2 %subtract_convert_fusion = bf16[8,256,512]{2,1,0:T(8,128)(2,1)} fusion(bf16[8,256,512]{2,1,0:T(8,128)(2,1)} %all-to-all-done.1, bf16[8,256,512]{2,1,0:T(8,128)(2,1)} %param.8), kind=kLoop, calls=%fused_computation.3 | loop fusion | flops 5242880 | bytes 6291456 | tf_op jit(solution)/shard_map/convert_element_type | solution.py:58
  173.8 3.6 %gather_fusion = bf16[8,256,512]{2,1,0:T(8,128)(2,1)} fusion(bf16[8,256,512]{2,1,0:T(8,128)(2,1)} %subtract_convert_fusion, s32[1024]{0:T(1024)S(1)} %pad_clamp_fusion.1), kind=kCustom, calls=%fused_computation.clone | custom fusion | bytes 4194336 | tf_op jit(solution)/shard_map/jit(_take)/gather | solution.py:71
  177.3 3.6 %gather_fusion.1 = bf16[8,256,512]{2,1,0:T(8,128)(2,1)} fusion(bf16[8,256,512]{2,1,0:T(8,128)(2,1)} %subtract_convert_fusion, s32[1024]{0:T(1024)S(1)} %pad_clamp_fusion), kind=kCustom, calls=%fused_computation.1.clone | custom fusion | bytes 4194336 | tf_op jit(solution)/shard_map/jit(_take)/gather | solution.py:71
  180.9 4.8 %select_select_fusion = (bf16[8,256,512]{2,1,0:T(8,128)(2,1)}, bf16[8,256,512]{2,1,0:T(8,128)(2,1)}) fusion(bf16[8,256,512]{2,1,0:T(8,128)(2,1)} %gather_fusion.1, pred[8]{0:T(512)(128)(4,1)S(1)} %get-tuple-element.3, pred[8]{0:T(512)(128)(4,1)S(1)} %get-tuple-element.9, bf16[8,256,512]{2,1,0:T(8,128)(2,1)} %gather_fusion, ...), kind=kLoop, calls=%fused_computation.12 | loop fusion | flops 4194304 | bytes 8388640 | tf_op jit(solution)/shard_map/jit(_where)/select_n | solution.py:72
  185.7 3.9 %copy.22 = bf16[8,256,512]{1,2,0:T(8,128)(2,1)} copy(bf16[8,256,512]{2,1,0:T(8,128)(2,1)} %get-tuple-element.12) | data formatting | bytes 4194304 | tf_op jit(solution)/shard_map/reshape | solution.py:73
  189.6 3.9 %copy.23 = bf16[8,256,512]{1,2,0:T(8,128)(2,1)} copy(bf16[8,256,512]{2,1,0:T(8,128)(2,1)} %get-tuple-element.11) | data formatting | bytes 4194304 | tf_op jit(solution)/shard_map/reshape | solution.py:73
  193.5 0.0 all-gather.2.cloned.1.call-done
  193.5 0.0 copy-start.1
  193.5 0.0 copy-start.2
  193.5 3.4 %fusion.2 = f32[8,4,128,384]{3,2,1,0:T(8,128)S(1)} fusion(bf16[8,256,4,128]{1,3,2,0:T(8,128)(2,1)} %bitcast.74, bf16[8,384,256]{2,1,0:T(8,128)(2,1)} %all-gather.2.cloned.1.call-done), kind=kOutput, calls=%fused_computation.15 | convolution fusion | flops 805306368 | bytes 9961472 | tf_op jit(solution)/shard_map/bti,bigc->gbtc/dot_general | solution.py:74
  197.0 0.0 copy-done.1
  197.0 0.0 copy-done.2
  197.0 2.9 fusion
  199.9 4.7 %copy.19 = bf16[4,8,384,128]{3,2,1,0:T(8,128)(2,1)} copy(bf16[4,8,384,128]{2,3,0,1:T(8,128)(2,1)} %fusion) | data formatting | bytes 6291456 | tf_op jit(solution)/shard_map/convert_element_type | solution.py:75
  204.6 0.0 reduce-scatter.2.cloned.1.call-update
  205.3 102.7 %reduce-scatter.2.cloned.1.call-done = bf16[1,384,128]{2,1,0:T(8,128)(2,1)} async-done(((bf16[32,384,128]{2,1,0:T(8,128)(2,1)}), bf16[1,384,128]{2,1,0:T(8,128)(2,1)}) %reduce-scatter.2.cloned.1.call-update) | async-done | bytes 98320 | tf_op jit(solution)/shard_map/reduce_scatter | solution.py:77
  307.9 1.7 bitcast_select_fusion
  (8 shorter events, 0.1 us)
Async XLA Ops:
  7.2 10.1 %copy-start = (bf16[384,2048]{1,0:T(8,128)(2,1)S(1)}, bf16[384,2048]{1,0:T(8,128)(2,1)}, u32[]{:S(2)}) copy-start(bf16[384,2048]{1,0:T(8,128)(2,1)} %param.10) | copy-start | bytes 4718596
  11.0 52.0 %all-to-all-start = ((bf16[8,256,512]{2,1,0:T(8,128)(2,1)}), bf16[8,256,512]{2,1,0:T(8,128)(2,1)}, u32[]{:S(2)}, u32[]{:S(2)}) async-start(bf16[8,256,512]{2,1,0:T(8,128)(2,1)} %clamp_convert_fusion), calls=%async_computation | async-start | bytes 4194304 | tf_op jit(solution)/shard_map/all_to_all | solution.py:45
  63.1 54.3 %all-to-all-start.2 = ((bf16[8,96,256]{2,1,0:T(8,128)(2,1)}), bf16[8,96,256]{2,1,0:T(8,128)(2,1)S(1)}, u32[]{:S(2)}, u32[]{:S(2)}) async-start(bf16[8,96,256]{2,1,0:T(8,128)(2,1)} %bitcast.71), calls=%async_computation.2 | async-start | bytes 786432 | tf_op jit(solution)/shard_map/all_to_all | solution.py:51
  117.4 0.8 copy-start.3
  117.4 7.7 %copy-start.4 = (s32[8,1]{0,1:T(1,128)S(1)}, s32[8,1]{0,1:T(1,128)}, u32[]{:S(2)}) copy-start(s32[8,1]{0,1:T(1,128)} %param.9) | copy-start | bytes 100
  118.1 51.4 %all-to-all-start.1 = ((bf16[8,256,512]{2,1,0:T(8,128)(2,1)}), bf16[8,256,512]{2,1,0:T(8,128)(2,1)}, u32[]{:S(2)}, u32[]{:S(2)}) async-start(bf16[8,256,512]{2,1,0:T(8,128)(2,1)} %bitcast.76), calls=%async_computation.1 | async-start | bytes 4194304 | tf_op jit(solution)/shard_map/all_to_all | solution.py:55
  124.1 69.4 %all-gather.2.cloned.1.call-start = ((), (), s32[]{:S(2)}) async-start(), calls=%async_computation.4 | async-start | bytes 1966080 | tf_op jit(solution)/shard_map/all_gather | solution.py:52
  124.9 183.1 %reduce-scatter.2.cloned.1.call-start = ((), (), s32[]{:S(2)}) async-start(), calls=%async_computation.5 | async-start | bytes 3244032 | tf_op jit(solution)/shard_map/reduce_scatter | solution.py:77
  193.5 3.5 %copy-start.1 = (bf16[8,256,512]{1,2,0:T(8,128)(2,1)S(1)}, bf16[8,256,512]{1,2,0:T(8,128)(2,1)}, u32[]{:S(2)}) copy-start(bf16[8,256,512]{1,2,0:T(8,128)(2,1)} %copy.23) | copy-start | bytes 6291460
  193.5 3.5 %copy-start.2 = (bf16[8,384,256]{2,1,0:T(8,128)(2,1)S(1)}, bf16[8,384,256]{2,1,0:T(8,128)(2,1)}, u32[]{:S(2)}) copy-start(bf16[8,384,256]{2,1,0:T(8,128)(2,1)} %all-gather.2.cloned.1.call-done) | copy-start | bytes 4718596
Sparse Core Ops, SparseCore 0:
  126.5 20.5 all-gather.1
  204.7 103.1 reduce-scatter.1

commit v2 on v1

v2 whole, which is shorter than its diff:
```python
import functools

import jax
import jax.numpy as jnp
from jax import lax
from jax.experimental import pallas as pl
from jax.experimental.pallas import tpu as pltpu
from jax.sharding import PartitionSpec as P

ITERS = 5
MOST = 2
CORES = 2

coef_a = 3.4445
coef_b = -4.775
coef_c = 2.0315
step_size = 0.5

f32 = jnp.float32
bf16 = jnp.bfloat16
MESH = pl.DeviceIdType.MESH


def far_first(n):
    return sorted(range(1, n), key=lambda k: abs(k - n // 2))


def greet(n, groups, grp_shifts):
    row, grp = lax.axis_index("row"), lax.axis_index("grp")
    barrier = pltpu.get_barrier_semaphore()
    for k in range(1, n):
        pl.semaphore_signal(
            barrier, inc=1, device_id=(grp, lax.rem(row + k, n)), device_id_type=MESH
        )
    for g in grp_shifts:
        pl.semaphore_signal(barrier, inc=1, device_id=(g, row), device_id_type=MESH)
    pl.semaphore_wait(barrier, n - 1 + len(grp_shifts))


def ortho_kernel(
    n, groups, raw, mine, back, cols, x, acc, gram, poly, ssem, rsem, tss, trs, gss, grs, bss, brs
):
    row, grp = lax.axis_index("row"), lax.axis_index("grp")
    width = raw.shape[2]
    others = [lax.rem(grp + k, groups) for k in range(1, groups)]
    greet(n, groups, others)
    order = far_first(n)

    def remote(src, dst, ss, rs, where):
        return pltpu.make_async_remote_copy(
            src_ref=src, dst_ref=dst, send_sem=ss, recv_sem=rs, device_id=where, device_id_type=MESH
        )

    sends, tsends = {}, {}
    for k in order:
        to = lax.rem(row + k, n)
        sends[k] = remote(raw.at[to], x.at[row], ssem.at[k], rsem.at[k], (grp, to))
        sends[k].start()
    for k in order:
        to = lax.rem(row + k, n)
        tsends[k] = remote(mine.at[to], cols.at[grp, row], tss.at[k], trs.at[k], (grp, to))
        tsends[k].start()

    def self_dot(v):
        return lax.dot_general(v, v, (((0,), (0,)), ((), ())), preferred_element_type=f32)

    x[row] = raw[row]
    cols[grp, row] = mine[row]
    acc[...] = self_dot(raw[row])
    for k in reversed(order):
        sends[k].wait_recv()
        acc[...] += self_dot(x[lax.rem(row + n - k, n)])

    total = acc[...]
    eye = lax.broadcasted_iota(jnp.int32, total.shape, 0) == lax.broadcasted_iota(
        jnp.int32, total.shape, 1
    )
    norm2 = jnp.sum(jnp.where(eye, total, 0.0), keepdims=True)
    scale = 1.0 / (jnp.sqrt(norm2) + 1e-07)
    acc[...] = jnp.where(norm2 < jnp.inf, scale * (scale * total), 0.0)

    gsends = []
    for turn in range(ITERS):
        first, last = turn == 0, turn == ITERS - 1
        gram[...] = acc[...].astype(bf16)
        square = jnp.dot(gram[...], gram[...], preferred_element_type=f32)
        poly[...] = (coef_b * gram[...].astype(f32) + coef_c * square).astype(bf16)

        def fresh(i):
            block = x[i]
            update = jnp.dot(block, poly[...], preferred_element_type=f32)
            if first:
                return ((coef_a * scale) * block.astype(f32) + scale * update).astype(bf16)
            return (coef_a * block.astype(f32) + update).astype(bf16)

        if not last:
            acc[...] = jnp.zeros_like(acc)

            def step(i, carry):
                block = fresh(i)
                x[i] = block
                acc[...] += self_dot(block)
                return carry

            lax.fori_loop(0, n, step, 0)
        if first:
            for k in order:
                tsends[k].wait_recv()
            for j, g in enumerate(others):
                copy = remote(cols.at[grp], cols.at[grp], gss.at[j], grs.at[j], (g, row))
                copy.start()
                gsends.append(copy)
        if last:
            bsends = {}
            for k in order:
                to = lax.rem(row + k, n)
                x[to] = fresh(to)
                bsends[k] = remote(x.at[to], back.at[row], bss.at[k], brs.at[k], (grp, to))
                bsends[k].start()
            back[row] = fresh(row)
    for k in order:
        sends[k].wait_send()
        tsends[k].wait_send()
    for copy in gsends:
        copy.wait()
    for k in order:
        bsends[k].wait()


def project_kernel(
    n, groups, index, valid, cols, fresh, out, part, got1, sum1, got2, sum2, got3,
    ss1, rs1, ss2, rs2, ss3, rs3
):
    row, grp = lax.axis_index("row"), lax.axis_index("grp")
    ys = groups // CORES
    y, core = grp // CORES, lax.rem(grp, CORES)
    count, piece = out.shape
    partners = [y * CORES + (1 - core)]
    partners += [lax.rem(y + j, ys) * CORES + core for j in range(1, ys)]
    greet(n, groups, partners)
    order = far_first(n) + [0]

    def remote(src, dst, ss, rs, where):
        copy = pltpu.make_async_remote_copy(
            src_ref=src, dst_ref=dst, send_sem=ss, recv_sem=rs, device_id=where, device_id_type=MESH
        )
        copy.start()
        return copy

    one, two, three = {}, {}, {}

    def stage1(k):
        b = lax.rem(row + k, n)
        tok = cols[:, b].reshape(count, cols.shape[3])
        total = jnp.zeros((count, groups * piece), f32)
        for s in range(MOST):
            term = jnp.dot(tok, fresh[index[b, s]], preferred_element_type=f32)
            total = total + jnp.where(valid[b, s] > 0, term, 0.0)
        total = (total * groups ** (-0.5)).astype(bf16)
        for g in range(groups):
            part[k, g % CORES, g // CORES] = total[:, g * piece : (g + 1) * piece]
        one[k] = remote(part.at[k, 1 - core], got1.at[k], ss1.at[k], rs1.at[k], (partners[0], row))

    def stage2(k):
        one[k].wait_recv()
        two[k] = []
        for j in range(1, ys):
            to = lax.rem(y + j, ys)
            both = part[k, core, to].astype(f32) + got1[k, to].astype(f32)
            sum1[k, j] = both.astype(bf16)
            two[k].append(
                remote(sum1.at[k, j], got2.at[k, j], ss2.at[k, j], rs2.at[k, j], (partners[j], row))
            )

    def stage3(k):
        total = part[k, core, y].astype(f32) + got1[k, y].astype(f32)
        for j in range(1, ys):
            two[k][j - 1].wait_recv()
            total = total + got2[k, j].astype(f32)
        if k == 0:
            return total
        sum2[k] = total.astype(bf16)
        to = lax.rem(row + k, n)
        three[k] = remote(sum2.at[k], got3.at[k], ss3.at[k], rs3.at[k], (grp, to))

    final = None
    lag2, lag3 = 1, 3
    for i in range(n + lag3):
        if i < n:
            stage1(order[i])
        if lag2 <= i < n + lag2:
            stage2(order[i - lag2])
        if lag3 <= i < n + lag3:
            final = stage3(order[i - lag3])
    for k in reversed(order[:-1]):
        three[k].wait_recv()
        final = final + got3[k].astype(f32)
    out[...] = final.astype(bf16)
    for k in order:
        one[k].wait_send()
        for copy in two[k]:
            copy.wait_send()
        if k:
            three[k].wait_send()


VM = pl.BlockSpec(memory_space=pltpu.VMEM)
SM = pl.BlockSpec(memory_space=pltpu.SMEM)


def body(grad, weight, owner, tokens, counts):
    ranks = lax.axis_size("row")
    groups = lax.axis_size("grp")
    number, rows, width = grad.shape
    assert number == ranks
    ys = groups // CORES
    dma = pltpu.SemaphoreType.DMA
    top = float(jnp.finfo(bf16).max)
    raw = jnp.clip(grad, -top, top).astype(bf16)

    count = tokens.shape[0]
    share = count // groups
    mine = lax.dynamic_slice_in_dim(tokens, lax.axis_index("grp") * share, share, 0)
    mine = jnp.stack([mine[:, r * rows : (r + 1) * rows] for r in range(ranks)])

    back, cols = pl.pallas_call(
        functools.partial(ortho_kernel, ranks, groups),
        out_shape=[
            jax.ShapeDtypeStruct((ranks, rows, width), bf16),
            jax.ShapeDtypeStruct((groups, ranks, share, rows), bf16),
        ],
        in_specs=[VM, VM],
        out_specs=[VM, VM],
        scratch_shapes=[
            pltpu.VMEM((ranks, rows, width), bf16),
            pltpu.VMEM((width, width), f32),
            pltpu.VMEM((width, width), bf16),
            pltpu.VMEM((width, width), bf16),
        ]
        + [dma((ranks,))] * 4
        + [dma((groups,))] * 2
        + [dma((ranks,))] * 2,
        compiler_params=pltpu.CompilerParams(
            collective_id=0, has_side_effects=True, vmem_limit_bytes=48 * 1024 * 1024
        ),
        name="ortho",
    )(raw, mine)
    new_weight = (weight.astype(f32) - step_size * back.astype(f32)).astype(bf16)

    target = owner[:, 0]
    before = jnp.arange(number)[None, :] < jnp.arange(number)[:, None]
    same = target[None, :] == target[:, None]
    slot = jnp.sum((same & before).astype(jnp.int32), axis=1)
    hit = (target[None, None, :] == jnp.arange(ranks)[:, None, None]) & (
        slot[None, None, :] == jnp.arange(MOST)[None, :, None]
    )
    index = jnp.sum(hit * jnp.arange(number)[None, None, :], axis=2).astype(jnp.int32)
    valid = jnp.any(hit, axis=2).astype(jnp.int32)

    piece = width // groups
    summed = pl.pallas_call(
        functools.partial(project_kernel, ranks, groups),
        out_shape=jax.ShapeDtypeStruct((count, piece), bf16),
        in_specs=[SM, SM, VM, VM],
        out_specs=VM,
        scratch_shapes=[
            pltpu.VMEM((ranks, CORES, ys, count, piece), bf16),
            pltpu.VMEM((ranks, ys, count, piece), bf16),
            pltpu.VMEM((ranks, ys, count, piece), bf16),
            pltpu.VMEM((ranks, ys, count, piece), bf16),
            pltpu.VMEM((ranks, count, piece), bf16),
            pltpu.VMEM((ranks, count, piece), bf16),
            dma((ranks,)),
            dma((ranks,)),
            dma((ranks, ys)),
            dma((ranks, ys)),
            dma((ranks,)),
            dma((ranks,)),
        ],
        compiler_params=pltpu.CompilerParams(
            collective_id=1, has_side_effects=True, vmem_limit_bytes=48 * 1024 * 1024
        ),
        name="project",
    )(index, valid, cols, new_weight)
    live = jnp.arange(count)[:, None] < counts[0]
    mixed = jnp.where(live, summed, jnp.zeros_like(summed))
    return (new_weight, mixed)


def solution(mesh):
    placed = (
        P("grp", "row", None),
        P("grp", "row", None),
        P("grp", None),
        P("row", None),
        P("row"),
    )
    return jax.shard_map(
        body,
        mesh=mesh,
        in_specs=placed,
        out_specs=(P("grp", "row", None), P("row", "grp")),
        check_vma=False,
    )
```

time: 319 us -> 167 us (0.52)
  waiting for transfers between devices: 192 us -> 0 us
  Pallas kernels: 0 us -> 150 us
  matrix products: 49.8 us -> 0 us
  starting transfers between devices: 18.7 us -> 0 us
  between operations: 16.2 us -> 1.36 us
  other arithmetic: 18.3 us -> 4.34 us
  local copies, waits for them, and re-layouts: 21.2 us -> 8.64 us
    pallas_call x0 -> x2, Pallas kernels: none -> 150 us  [the longest x1 119 us: body(): pl.pallas_call(functools.partial(ortho_kernel, ranks, groups), out_shape=...]
    reduce_scatter x1 -> x0, waiting for transfers between devices: 103 us -> none  [body(): lax.psum_scatter(proj, ('grp', 'row'), scatter_dimension=0, tiled=True)[0]]
    all_to_all x3 -> x0, waiting for transfers between devices: 88.9 us -> none  [the longest x1 45 us: body(): whole = lax.all_to_all(raw, 'row', split_axis=0, concat_axis=0, tiled=True)]
    dot_general x12 -> x0, matrix products: 49.8 us -> none  [the longest x5 25.9 us: newton_schulz(): update = jnp.dot(state, poly, preferred_element_type=f32)]
    all_to_all x3 -> x0, starting transfers between devices: 18.4 us -> none  [the longest x1 6.25 us: body(): whole = lax.all_to_all(raw, 'row', split_axis=0, concat_axis=0, tiled=True)]
    reshape x3 -> x0, local copies, waits for them, and re-layouts: 8.56 us -> none  [the longest x2 7.79 us: body(): picked = picked.reshape(ranks, rows, groups, width // groups)]
    gather x2 -> x0, local copies, waits for them, and re-layouts: 7.16 us -> none  [body(): picked = jnp.take(new_weight, index[:, s], axis=0)]
    unnamed x10 -> x17, local copies, waits for them, and re-layouts: 0.78 us -> 7.66 us
  transfers between devices with their start and end apart: 5 -> 0, of which waited for: 3 -> 0; matrix products, arithmetic and copies ran while one was open for 23% -> 0% of each run, Pallas kernels for 0% -> 0%
where the time goes in v2:
time: 167 us; the launch traced here: 164 us
  Pallas kernels  150 us (90%)
  local copies, waits for them, and re-layouts  8.64 us (5%)
  other arithmetic  4.34 us (3%)
    pallas_call x1, Pallas kernels, body(): pl.pallas_call(functools.partial(ortho_kernel, ranks, groups), out_shape=...  119 us
    pallas_call x1, Pallas kernels, body(): pl.pallas_call(functools.partial(project_kernel, ranks, groups), out_shap...  30.7 us
    unnamed x17, local copies, waits for them, and re-layouts  7.66 us

profile of v2, /device:TPU:8, one launch (start us, length us, event | category | flops | bytes accessed | tf_op | source)
XLA Modules:
  0.0 164.4 jit_solution(9258593972261117138)
XLA Ops:
  0.6 0.8 fusion.7
  1.4 0.8 fusion.6
  2.2 0.8 fusion.5
  3.0 0.8 fusion.4
  3.8 0.8 fusion.3
  4.7 0.8 fusion.2
  5.5 0.8 fusion.1
  6.3 0.8 fusion.mine
  7.1 2.4 %clamp_convert_fusion.raw = bf16[8,256,512]{2,1,0:T(8,128)(2,1)S(1)} fusion(f32[8,256,512]{2,1,0:T(8,128)} %param.5), kind=kLoop, calls=%fused_computation.1 | loop fusion | flops 1048576 | bytes 6291456 | tf_op jit(solution)/shard_map/convert_element_type | solution.py:219
  9.5 0.0 copy-start.3
  9.5 119.4 %ortho.1 = (bf16[8,256,512]{2,1,0:T(8,128)(2,1)S(1)}, bf16[4,8,96,256]{3,2,1,0:T(8,128)(2,1)S(1)}) custom-call(bf16[8,256,512]{2,1,0:T(8,128)(2,1)S(1)} %clamp_convert_fusion.raw, bf16[8,96,256]{2,1,0:T(8,128)(2,1)S(1)} %fusion.mine), custom_call_target="tpu_custom_call" | custom-call | tf_op jit(solution)/shard_map/ortho/pallas_call | solution.py:226
  128.9 0.0 copy-start.1
  128.9 0.0 copy-done.3
  128.9 0.0 copy-start.4
  128.9 0.7 subtract_convert_fusion.fresh
  129.6 0.6 copy-done.1
  130.2 0.0 copy-start
  130.2 0.0 copy-done.4
  130.2 0.2 convert_reduce_fusion
  130.4 0.1 and_reduce_fusion
  130.5 0.1 copy.7
  130.6 0.2 fusion.8
  130.8 0.1 copy.8.index
  130.9 0.0 copy-start.2
  130.9 1.4 copy-done.2
  132.3 30.7 %project.1 = bf16[384,128]{1,0:T(8,128)(2,1)S(1)} custom-call(s32[8,2]{1,0:T(8,128)S(1)} %copy.8.index, s32[8,2]{1,0:T(8,128)S(1)} %convert_element_type.24.valid, bf16[4,8,96,256]{3,2,1,0:T(8,128)(2,1)S(1)} %copy-done.2, bf16[8,256,512]{2,1,0:T(8,128)(2,1)S(1)} %subtract_convert_fusion.fresh), custom_call_target="tpu_custom_call" | custom-call | tf_op jit(solution)/shard_map/project/pallas_call | solution.py:261
  163.7 0.8 broadcast_select_fusion
  164.4 0.0 copy-done
  (4 shorter events, 0.0 us)
Async XLA Ops:
  9.5 119.4 %copy-start.3 = (bf16[8,256,512]{2,1,0:T(8,128)(2,1)S(1)}, bf16[8,256,512]{2,1,0:T(8,128)(2,1)}, u32[]{:S(2)}) copy-start(bf16[8,256,512]{2,1,0:T(8,128)(2,1)} %param.6) | copy-start | bytes 6291460
  128.9 1.3 copy-start.1
  128.9 1.3 copy-start.4
  130.2 34.2 %copy-start = (bf16[8,256,512]{2,1,0:T(8,128)(2,1)}, bf16[8,256,512]{2,1,0:T(8,128)(2,1)S(1)}, u32[]{:S(2)}) copy-start(bf16[8,256,512]{2,1,0:T(8,128)(2,1)S(1)} %subtract_convert_fusion.fresh) | copy-start | bytes 6291460
  130.9 1.4 copy-start.2

commit v3 on v2

--- a/solution.py
+++ b/solution.py
@@ -37,8 +37,10 @@
     pl.semaphore_wait(barrier, n - 1 + len(grp_shifts))
 
 
-def ortho_kernel(
-    n, groups, raw, mine, back, cols, x, acc, gram, poly, ssem, rsem, tss, trs, gss, grs, bss, brs
+def whole_kernel(
+    n, groups, owner, index, valid, raw, tokens, weight, back, out, cols, x, acc, gram, poly,
+    prod, part, got1, sum1, got2, sum2, got3,
+    ssem, rsem, tss, trs, gss, grs, bss, brs, own_sem, ss1, rs1, ss2, rs2, ss3, rs3
 ):
     row, grp = lax.axis_index("row"), lax.axis_index("grp")
     width = raw.shape[2]
@@ -50,6 +52,11 @@
         return pltpu.make_async_remote_copy(
             src_ref=src, dst_ref=dst, send_sem=ss, recv_sem=rs, device_id=where, device_id_type=MESH
         )
+
+    def share_of(to):
+        size, wide = cols.shape[2], cols.shape[3]
+        down = pl.ds(pl.multiple_of(grp * size, size), size)
+        return tokens.at[down, pl.ds(pl.multiple_of(to * wide, wide), wide)]
 
     sends, tsends = {}, {}
     for k in order:
@@ -58,14 +65,15 @@
         sends[k].start()
     for k in order:
         to = lax.rem(row + k, n)
-        tsends[k] = remote(mine.at[to], cols.at[grp, row], tss.at[k], trs.at[k], (grp, to))
+        tsends[k] = remote(share_of(to), cols.at[grp, row], tss.at[k], trs.at[k], (grp, to))
         tsends[k].start()
 
     def self_dot(v):
         return lax.dot_general(v, v, (((0,), (0,)), ((), ())), preferred_element_type=f32)
 
     x[row] = raw[row]
-    cols[grp, row] = mine[row]
+    own = pltpu.make_async_copy(share_of(row), cols.at[grp, row], own_sem)
+    own.start()
     acc[...] = self_dot(raw[row])
     for k in reversed(order):
         sends[k].wait_recv()
@@ -104,6 +112,7 @@
 
             lax.fori_loop(0, n, step, 0)
         if first:
+            own.wait()
             for k in order:
                 tsends[k].wait_recv()
             for j, g in enumerate(others):
@@ -118,32 +127,28 @@
                 bsends[k] = remote(x.at[to], back.at[row], bss.at[k], brs.at[k], (grp, to))
                 bsends[k].start()
             back[row] = fresh(row)
-    for k in order:
-        sends[k].wait_send()
-        tsends[k].wait_send()
     for copy in gsends:
         copy.wait()
-    for k in order:
-        bsends[k].wait()
-
-
-def project_kernel(
-    n, groups, index, valid, cols, fresh, out, part, got1, sum1, got2, sum2, got3,
-    ss1, rs1, ss2, rs2, ss3, rs3
-):
-    row, grp = lax.axis_index("row"), lax.axis_index("grp")
+
+    def product(e):
+        fresh = (weight[e].astype(f32) - step_size * back[e].astype(f32)).astype(bf16)
+        tok = jnp.concatenate([cols[g, owner[e]] for g in range(groups)], axis=0)
+        prod[e] = jnp.dot(tok, fresh, preferred_element_type=f32)
+
+    product(row)
+    for k in reversed(order):
+        bsends[k].wait_recv()
+        product(lax.rem(row + n - k, n))
+
     ys = groups // CORES
     y, core = grp // CORES, lax.rem(grp, CORES)
     count, piece = out.shape
     partners = [y * CORES + (1 - core)]
     partners += [lax.rem(y + j, ys) * CORES + core for j in range(1, ys)]
-    greet(n, groups, partners)
-    order = far_first(n) + [0]
-
-    def remote(src, dst, ss, rs, where):
-        copy = pltpu.make_async_remote_copy(
-            src_ref=src, dst_ref=dst, send_sem=ss, recv_sem=rs, device_id=where, device_id_type=MESH
-        )
+    turns = order + [0]
+
+    def started(*args):
+        copy = remote(*args)
         copy.start()
         return copy
 
@@ -151,15 +156,13 @@
 
     def stage1(k):
         b = lax.rem(row + k, n)
-        tok = cols[:, b].reshape(count, cols.shape[3])
         total = jnp.zeros((count, groups * piece), f32)
         for s in range(MOST):
-            term = jnp.dot(tok, fresh[index[b, s]], preferred_element_type=f32)
-            total = total + jnp.where(valid[b, s] > 0, term, 0.0)
+            total = total + jnp.where(valid[b, s] > 0, prod[index[b, s]], 0.0)
         total = (total * groups ** (-0.5)).astype(bf16)
         for g in range(groups):
             part[k, g % CORES, g // CORES] = total[:, g * piece : (g + 1) * piece]
-        one[k] = remote(part.at[k, 1 - core], got1.at[k], ss1.at[k], rs1.at[k], (partners[0], row))
+        one[k] = started(part.at[k, 1 - core], got1.at[k], ss1.at[k], rs1.at[k], (partners[0], row))
 
     def stage2(k):
         one[k].wait_recv()
@@ -169,7 +172,7 @@
             both = part[k, core, to].astype(f32) + got1[k, to].astype(f32)
             sum1[k, j] = both.astype(bf16)
             two[k].append(
-                remote(sum1.at[k, j], got2.at[k, j], ss2.at[k, j], rs2.at[k, j], (partners[j], row))
+                started(sum1.at[k, j], got2.at[k, j], ss2.at[k, j], rs2.at[k, j], (partners[j], row))
             )
 
     def stage3(k):
@@ -181,27 +184,31 @@
             return total
         sum2[k] = total.astype(bf16)
         to = lax.rem(row + k, n)
-        three[k] = remote(sum2.at[k], got3.at[k], ss3.at[k], rs3.at[k], (grp, to))
+        three[k] = started(sum2.at[k], got3.at[k], ss3.at[k], rs3.at[k], (grp, to))
 
     final = None
     lag2, lag3 = 1, 3
     for i in range(n + lag3):
         if i < n:
-            stage1(order[i])
+            stage1(turns[i])
         if lag2 <= i < n + lag2:
-            stage2(order[i - lag2])
+            stage2(turns[i - lag2])
         if lag3 <= i < n + lag3:
-            final = stage3(order[i - lag3])
-    for k in reversed(order[:-1]):
+            final = stage3(turns[i - lag3])
+    for k in reversed(turns[:-1]):
         three[k].wait_recv()
         final = final + got3[k].astype(f32)
     out[...] = final.astype(bf16)
-    for k in order:
+    for k in turns:
         one[k].wait_send()
         for copy in two[k]:
             copy.wait_send()
         if k:
             three[k].wait_send()
+    for k in order:
+        sends[k].wait_send()
+        tsends[k].wait_send()
+        bsends[k].wait_send()
 
 
 VM = pl.BlockSpec(memory_space=pltpu.VMEM)
@@ -220,33 +227,6 @@
 
     count = tokens.shape[0]
     share = count // groups
-    mine = lax.dynamic_slice_in_dim(tokens, lax.axis_index("grp") * share, share, 0)
-    mine = jnp.stack([mine[:, r * rows : (r + 1) * rows] for r in range(ranks)])
-
-    back, cols = pl.pallas_call(
-        functools.partial(ortho_kernel, ranks, groups),
-        out_shape=[
-            jax.ShapeDtypeStruct((ranks, rows, width), bf16),
-            jax.ShapeDtypeStruct((groups, ranks, share, rows), bf16),
-        ],
-        in_specs=[VM, VM],
-        out_specs=[VM, VM],
-        scratch_shapes=[
-            pltpu.VMEM((ranks, rows, width), bf16),
-            pltpu.VMEM((width, width), f32),
-            pltpu.VMEM((width, width), bf16),
-            pltpu.VMEM((width, width), bf16),
-        ]
-        + [dma((ranks,))] * 4
-        + [dma((groups,))] * 2
-        + [dma((ranks,))] * 2,
-        compiler_params=pltpu.CompilerParams(
-            collective_id=0, has_side_effects=True, vmem_limit_bytes=48 * 1024 * 1024
-        ),
-        name="ortho",
-    )(raw, mine)
-    new_weight = (weight.astype(f32) - step_size * back.astype(f32)).astype(bf16)
-
     target = owner[:, 0]
     before = jnp.arange(number)[None, :] < jnp.arange(number)[:, None]
     same = target[None, :] == target[:, None]
@@ -258,30 +238,41 @@
     valid = jnp.any(hit, axis=2).astype(jnp.int32)
 
     piece = width // groups
-    summed = pl.pallas_call(
-        functools.partial(project_kernel, ranks, groups),
-        out_shape=jax.ShapeDtypeStruct((count, piece), bf16),
-        in_specs=[SM, SM, VM, VM],
-        out_specs=VM,
+    back, summed = pl.pallas_call(
+        functools.partial(whole_kernel, ranks, groups),
+        out_shape=[
+            jax.ShapeDtypeStruct((ranks, rows, width), bf16),
+            jax.ShapeDtypeStruct((count, piece), bf16),
+        ],
+        in_specs=[SM, SM, SM, VM, pl.BlockSpec(memory_space=pl.ANY), VM],
+        out_specs=[VM, VM],
         scratch_shapes=[
+            pltpu.VMEM((groups, ranks, share, rows), bf16),
+            pltpu.VMEM((ranks, rows, width), bf16),
+            pltpu.VMEM((width, width), f32),
+            pltpu.VMEM((width, width), bf16),
+            pltpu.VMEM((width, width), bf16),
+            pltpu.VMEM((ranks, count, width), f32),
             pltpu.VMEM((ranks, CORES, ys, count, piece), bf16),
             pltpu.VMEM((ranks, ys, count, piece), bf16),
             pltpu.VMEM((ranks, ys, count, piece), bf16),
             pltpu.VMEM((ranks, ys, count, piece), bf16),
             pltpu.VMEM((ranks, count, piece), bf16),
             pltpu.VMEM((ranks, count, piece), bf16),
-            dma((ranks,)),
-            dma((ranks,)),
-            dma((ranks, ys)),
-            dma((ranks, ys)),
-            dma((ranks,)),
-            dma((ranks,)),
-        ],
+        ]
+        + [dma((ranks,))] * 4
+        + [dma((groups,))] * 2
+        + [dma((ranks,))] * 2
+        + [dma]
+        + [dma((ranks,))] * 2
+        + [dma((ranks, ys))] * 2
+        + [dma((ranks,))] * 2,
         compiler_params=pltpu.CompilerParams(
-            collective_id=1, has_side_effects=True, vmem_limit_bytes=48 * 1024 * 1024
+            collective_id=0, has_side_effects=True, vmem_limit_bytes=60 * 1024 * 1024
         ),
-        name="project",
-    )(index, valid, cols, new_weight)
+        name="whole",
+    )(target, index, valid, raw, tokens, weight)
+    new_weight = (weight.astype(f32) - step_size * back.astype(f32)).astype(bf16)
     live = jnp.arange(count)[:, None] < counts[0]
     mixed = jnp.where(live, summed, jnp.zeros_like(summed))
     return (new_weight, mixed)

time: 167 us -> 172 us (1.030); the launches traced: 164 us -> 172 us
  Pallas kernels: 150 us -> 159 us
  local copies, waits for them, and re-layouts: 8.64 us -> 0.79 us
  other arithmetic: 4.34 us -> 10.6 us
    pallas_call x2 -> x1, Pallas kernels: 150 us -> 159 us  [body(): pl.pallas_call(functools.partial(whole_kernel, ranks, groups), out_shape=...]
    unnamed x17 -> x4, local copies, waits for them, and re-layouts: 7.66 us -> 0.01 us
    convert_element_type x1, other arithmetic: 0.65 us -> 3.65 us  [body(): (weight.astype(f32) - step_size * back.astype(f32)).astype(bf16)]
where the time goes in v3:
time: 172 us
  Pallas kernels  159 us (92%)
  other arithmetic  10.6 us (6%)
    pallas_call x1, Pallas kernels, body(): pl.pallas_call(functools.partial(whole_kernel, ranks, groups), out_shape=...  159 us
    convert_element_type x1, other arithmetic, body(): raw = jnp.clip(grad, -top, top).astype(bf16)  3.74 us
    convert_element_type x1, other arithmetic, body(): (weight.astype(f32) - step_size * back.astype(f32)).astype(bf16)  3.65 us

profile of v3, /device:TPU:8, one launch (start us, length us, event | category | flops | bytes accessed | tf_op | source)
XLA Modules:
  0.0 172.2 jit_solution(11023893683936994641)
XLA Ops:
  0.6 0.7 iota_compare_fusion.1
  1.3 0.9 convert_reduce_fusion
  2.2 0.1 and_reduce_fusion
  2.4 0.1 copy.7
  2.5 0.6 convert_element_type.21.valid
  3.1 0.1 fusion
  3.2 0.7 copy.8.index
  3.9 3.7 %clamp_convert_fusion.raw = bf16[8,256,512]{2,1,0:T(8,128)(2,1)} fusion(f32[8,256,512]{2,1,0:T(8,128)} %param.5), kind=kLoop, calls=%fused_computation.1 | loop fusion | flops 1048576 | bytes 6291456 | tf_op jit(solution)/shard_map/convert_element_type | solution.py:226
  7.6 0.0 copy-start
  7.6 159.4 %whole.1 = (bf16[8,256,512]{2,1,0:T(8,128)(2,1)}, bf16[384,128]{1,0:T(8,128)(2,1)}) custom-call(s32[8]{0:T(128)} %bitcast.5, s32[8,2]{1,0:T(8,128)} %copy.8.index, s32[8,2]{1,0:T(8,128)} %convert_element_type.21.valid, bf16[8,256,512]{2,1,0:T(8,128)(2,1)} %clamp_convert_fusion.raw, bf16[384,2048]{1,0:T(8,128)(2,1)} %tokens.1, bf16[8,256,512]{2,1,0:T(8,128)(2,1)} %weight.1), custom_call_target="tpu_custom_call" | custom-call | tf_op jit(solution)/shard_map/whole/pallas_call | solution.py:241
  167.1 0.0 copy-start.1
  167.1 0.0 copy-done
  167.1 3.6 %subtract_convert_fusion = bf16[8,256,512]{2,1,0:T(8,128)(2,1)} fusion(bf16[8,256,512]{2,1,0:T(8,128)(2,1)} %get-tuple-element.4, bf16[8,256,512]{2,1,0:T(8,128)(2,1)S(1)} %copy-done), kind=kLoop, calls=%fused_computation | loop fusion | flops 5242880 | bytes 6291456 | tf_op jit(solution)/shard_map/convert_element_type | solution.py:275
  171.4 0.0 copy-done.1
  171.4 0.8 broadcast_select_fusion
  (2 shorter events, 0.0 us)
Async XLA Ops:
  7.6 159.5 %copy-start = (bf16[8,256,512]{2,1,0:T(8,128)(2,1)S(1)}, bf16[8,256,512]{2,1,0:T(8,128)(2,1)}, u32[]{:S(2)}) copy-start(bf16[8,256,512]{2,1,0:T(8,128)(2,1)} %weight.1) | copy-start | bytes 6291460
  167.1 4.3 %copy-start.1 = (bf16[384,128]{1,0:T(8,128)(2,1)S(1)}, bf16[384,128]{1,0:T(8,128)(2,1)}, u32[]{:S(2)}) copy-start(bf16[384,128]{1,0:T(8,128)(2,1)} %get-tuple-element.5) | copy-start | bytes 294916

commit v4 on v2

--- a/solution.py
+++ b/solution.py
@@ -10,6 +10,7 @@
 ITERS = 5
 MOST = 2
 CORES = 2
+LAGS = (1, 3)
 
 coef_a = 3.4445
 coef_b = -4.775
@@ -38,7 +39,7 @@
 
 
 def ortho_kernel(
-    n, groups, raw, mine, back, cols, x, acc, gram, poly, ssem, rsem, tss, trs, gss, grs, bss, brs
+    n, groups, raw, tokens, back, cols, x, acc, gram, poly, ssem, rsem, tss, trs, gss, grs, bss, brs, own_sem
 ):
     row, grp = lax.axis_index("row"), lax.axis_index("grp")
     width = raw.shape[2]
@@ -51,6 +52,11 @@
             src_ref=src, dst_ref=dst, send_sem=ss, recv_sem=rs, device_id=where, device_id_type=MESH
         )
 
+    def share_of(to):
+        size, wide = cols.shape[2], cols.shape[3]
+        down = pl.ds(pl.multiple_of(grp * size, size), size)
+        return tokens.at[down, pl.ds(pl.multiple_of(to * wide, wide), wide)]
+
     sends, tsends = {}, {}
     for k in order:
         to = lax.rem(row + k, n)
@@ -58,14 +64,15 @@
         sends[k].start()
     for k in order:
         to = lax.rem(row + k, n)
-        tsends[k] = remote(mine.at[to], cols.at[grp, row], tss.at[k], trs.at[k], (grp, to))
+        tsends[k] = remote(share_of(to), cols.at[grp, row], tss.at[k], trs.at[k], (grp, to))
         tsends[k].start()
 
     def self_dot(v):
         return lax.dot_general(v, v, (((0,), (0,)), ((), ())), preferred_element_type=f32)
 
     x[row] = raw[row]
-    cols[grp, row] = mine[row]
+    own = pltpu.make_async_copy(share_of(row), cols.at[grp, row], own_sem)
+    own.start()
     acc[...] = self_dot(raw[row])
     for k in reversed(order):
         sends[k].wait_recv()
@@ -104,6 +111,7 @@
 
             lax.fori_loop(0, n, step, 0)
         if first:
+            own.wait()
             for k in order:
                 tsends[k].wait_recv()
             for j, g in enumerate(others):
@@ -184,7 +192,7 @@
         three[k] = remote(sum2.at[k], got3.at[k], ss3.at[k], rs3.at[k], (grp, to))
 
     final = None
-    lag2, lag3 = 1, 3
+    lag2, lag3 = LAGS
     for i in range(n + lag3):
         if i < n:
             stage1(order[i])
@@ -220,16 +228,13 @@
 
     count = tokens.shape[0]
     share = count // groups
-    mine = lax.dynamic_slice_in_dim(tokens, lax.axis_index("grp") * share, share, 0)
-    mine = jnp.stack([mine[:, r * rows : (r + 1) * rows] for r in range(ranks)])
-
     back, cols = pl.pallas_call(
         functools.partial(ortho_kernel, ranks, groups),
         out_shape=[
             jax.ShapeDtypeStruct((ranks, rows, width), bf16),
             jax.ShapeDtypeStruct((groups, ranks, share, rows), bf16),
         ],
-        in_specs=[VM, VM],
+        in_specs=[VM, pl.BlockSpec(memory_space=pl.ANY)],
         out_specs=[VM, VM],
         scratch_shapes=[
             pltpu.VMEM((ranks, rows, width), bf16),
@@ -239,12 +244,13 @@
         ]
         + [dma((ranks,))] * 4
         + [dma((groups,))] * 2
-        + [dma((ranks,))] * 2,
+        + [dma((ranks,))] * 2
+        + [dma],
         compiler_params=pltpu.CompilerParams(
             collective_id=0, has_side_effects=True, vmem_limit_bytes=48 * 1024 * 1024
         ),
         name="ortho",
-    )(raw, mine)
+    )(raw, tokens)
     new_weight = (weight.astype(f32) - step_size * back.astype(f32)).astype(bf16)
 
     target = owner[:, 0]

time: 167 us -> 163 us (0.976)
  local copies, waits for them, and re-layouts: 8.64 us -> 2.23 us
  Pallas kernels: 150 us -> 152 us
    unnamed x17 -> x12, local copies, waits for them, and re-layouts: 7.66 us -> 2.05 us
where the time goes in v4:
time: 163 us; the launch traced here: 161 us
  Pallas kernels  152 us (93%)
  other arithmetic  5.79 us (4%)
  local copies, waits for them, and re-layouts  2.23 us (1%)
    pallas_call x1, Pallas kernels, body(): pl.pallas_call(functools.partial(ortho_kernel, ranks, groups), out_shape=...  121 us
    pallas_call x1, Pallas kernels, body(): pl.pallas_call(functools.partial(project_kernel, ranks, groups), out_shap...  30.7 us
    convert_element_type x1, other arithmetic, body(): raw = jnp.clip(grad, -top, top).astype(bf16)  3.86 us

profile of v4, /device:TPU:8, one launch (start us, length us, event | category | flops | bytes accessed | tf_op | source)
XLA Modules:
  0.0 161.1 jit_solution(2354201790703311650)
XLA Ops:
  0.6 0.0 copy-start.1
  0.6 3.9 %clamp_convert_fusion.raw = bf16[8,256,512]{2,1,0:T(8,128)(2,1)} fusion(f32[8,256,512]{2,1,0:T(8,128)} %param.5), kind=kLoop, calls=%fused_computation.1 | loop fusion | flops 1048576 | bytes 6291456 | tf_op jit(solution)/shard_map/convert_element_type | solution.py:227
  4.5 0.0 copy-done.1
  4.5 0.0 copy-start.4
  4.5 121.0 %ortho.1 = (bf16[8,256,512]{2,1,0:T(8,128)(2,1)S(1)}, bf16[4,8,96,256]{3,2,1,0:T(8,128)(2,1)S(1)}) custom-call(bf16[8,256,512]{2,1,0:T(8,128)(2,1)} %clamp_convert_fusion.raw, bf16[384,2048]{1,0:T(8,128)(2,1)S(1)} %copy-done.1), custom_call_target="tpu_custom_call" | custom-call | tf_op jit(solution)/shard_map/ortho/pallas_call | solution.py:231
  125.5 0.0 copy-start.2
  125.5 0.0 copy-done.4
  125.5 0.0 copy-start.5
  125.6 0.7 subtract_convert_fusion.fresh
  126.2 0.6 copy-done.2
  126.8 0.0 copy-start
  126.8 0.0 copy-done.5
  126.8 0.2 convert_reduce_fusion
  127.0 0.1 fusion
  127.2 0.1 copy.8.index
  127.3 0.2 and_reduce_fusion
  127.4 0.1 copy.7
  127.5 0.0 copy-start.3
  127.5 1.4 copy-done.3
  128.9 30.7 %project.1 = bf16[384,128]{1,0:T(8,128)(2,1)S(1)} custom-call(s32[8,2]{1,0:T(8,128)S(1)} %copy.8.index, s32[8,2]{1,0:T(8,128)S(1)} %convert_element_type.24.valid, bf16[4,8,96,256]{3,2,1,0:T(8,128)(2,1)S(1)} %copy-done.3, bf16[8,256,512]{2,1,0:T(8,128)(2,1)S(1)} %subtract_convert_fusion.fresh), custom_call_target="tpu_custom_call" | custom-call | tf_op jit(solution)/shard_map/project/pallas_call | solution.py:267
  160.3 0.8 broadcast_select_fusion
  161.1 0.0 copy-done
  (4 shorter events, 0.0 us)
Async XLA Ops:
  0.6 3.9 %copy-start.1 = (bf16[384,2048]{1,0:T(8,128)(2,1)S(1)}, bf16[384,2048]{1,0:T(8,128)(2,1)}, u32[]{:S(2)}) copy-start(bf16[384,2048]{1,0:T(8,128)(2,1)} %tokens.1) | copy-start | bytes 4718596
  4.5 121.0 %copy-start.4 = (bf16[8,256,512]{2,1,0:T(8,128)(2,1)S(1)}, bf16[8,256,512]{2,1,0:T(8,128)(2,1)}, u32[]{:S(2)}) copy-start(bf16[8,256,512]{2,1,0:T(8,128)(2,1)} %param.6) | copy-start | bytes 6291460
  125.5 1.3 copy-start.2
  125.5 1.3 copy-start.5
  126.8 34.3 %copy-start = (bf16[8,256,512]{2,1,0:T(8,128)(2,1)}, bf16[8,256,512]{2,1,0:T(8,128)(2,1)S(1)}, u32[]{:S(2)}) copy-start(bf16[8,256,512]{2,1,0:T(8,128)(2,1)S(1)} %subtract_convert_fusion.fresh) | copy-start | bytes 6291460
  127.5 1.4 copy-start.3
